TPU v7x, 128 devices: a whole 4x4x4 slice. The times are simulated.
128 devices in a mesh: row: 32 (over x, y, core), col: 4 (over z).
Axes of the slice: x: 4, y: 4, z: 4, core: 2. Of those that a mesh axis runs over, the one named last changes fastest.
Arguments:
- right_side: bfloat16 [65536, 4096], P(('row', 'col')), may hold values from -6 to 6
- factor: bfloat16 [65536, 2048], P(('row', 'col')), may hold values from -0.125 to 0.125
- diag_inverse: bfloat16 [2048, 512], P('col'), as said below
- tile_mask: int32 [128, 4], P(('row', 'col')), may hold values from 0 to 1, as said below
- window_rows: int32 [4], replicated, may hold values from 0 to 127, as said below
Outputs:
- solution: bfloat16 [2048, 4096], P('row', 'col')
- updated_rhs: bfloat16 [65536, 4096], P(('row', 'col'))
Inputs may be any that keep to these rules, and one draw needn't show every extreme that they name: `window_rows`: distinct stored panel numbers, panels 0 and 127 always among them; panel p is stored on device p // 1 of row+col, and the window panels lie on different devices. `tile_mask`: 0 or 1; in the row of window panel k the entries of columns k and beyond are 0. `diag_inverse`: each tile is lower triangular.
All inputs are finite; a program needn't handle non-finite values.
Results may differ from a plain program's by a relative error of at most 0.0056.
Values may be sent and summed in bfloat16 or wider, within the bound.
A program may use at most 128 MiB of HBM per device.

v0:
```python
import jax
import jax.numpy as jnp
from jax import lax
from jax.sharding import PartitionSpec as P

AXES = ("row", "col")
NT = (((1,), (1,)), ((), ()))


def dot_nt(a, b):
    return lax.dot_general(a, b, NT, preferred_element_type=jnp.float32)


def body(right_side, factor, diag_inverse, tile_mask, window_rows):
    panel = diag_inverse.shape[1]
    window = factor.shape[1] // panel
    columns = right_side.shape[1]
    ncol = lax.axis_size("col")
    nrow = lax.axis_size("row")
    ndev = nrow * ncol
    width = columns // ndev
    col_index = lax.axis_index("col")
    row_index = lax.axis_index("row")
    me = row_index * ncol + col_index
    present = jnp.repeat(tile_mask[0] > 0, panel)
    masked = jnp.where(present[None, :], factor, jnp.zeros_like(factor))
    pieces = lax.all_to_all(
        right_side.T.reshape(ndev, width, panel), AXES, split_axis=0, concat_axis=0, tiled=True
    )
    lower = []
    for k in range(1, window):
        mine = me == window_rows[k]
        for j in range(k):
            tile = masked[:, j * panel : (j + 1) * panel]
            lower.append(jnp.where(mine, tile, jnp.zeros_like(tile)))
    lower = lax.psum(jnp.stack(lower), AXES)
    inverses = lax.all_gather(diag_inverse, "col", axis=0, tiled=True).reshape(window, panel, panel)
    solved = []
    for k in range(window):
        residual = lax.dynamic_index_in_dim(pieces, window_rows[k], 0, keepdims=False).astype(
            jnp.float32
        )
        for j in range(k):
            residual = residual - dot_nt(solved[j], lower[k * (k - 1) // 2 + j])
        solved.append(dot_nt(residual.astype(jnp.bfloat16), inverses[k]).astype(jnp.bfloat16))
    whole = lax.all_gather(jnp.concatenate(solved, axis=1), AXES, axis=0, tiled=True)
    updated = (right_side.astype(jnp.float32) - dot_nt(masked, whole)).astype(jnp.bfloat16)
    block_rows = window * panel // nrow
    block_cols = columns // ncol
    solution = lax.dynamic_slice(
        whole, (col_index * block_cols, row_index * block_rows), (block_cols, block_rows)
    ).T
    return (solution, updated)


def solution(mesh):
    in_specs = (P(AXES, None), P(AXES, None), P("col", None), P(AXES, None), P())
    out_specs = (P("row", "col"), P(AXES, None))
    return jax.shard_map(body, mesh=mesh, in_specs=in_specs, out_specs=out_specs, check_vma=False)
```

profile of v0, /device:TPU:1, one launch (start us, length us, event | category | flops | bytes accessed | tf_op | source)
XLA Modules:
  0.0 338.8 jit_solution(7828299529200578639)
XLA Ops:
  8.0 0.0 all-gather.3.cloned.1.call-start
  8.0 0.7 all-gather.3.cloned.1.call-update
  8.7 6.4 %copy.8 = bf16[512,4096]{0,1:T(8,128)(2,1)} copy(bf16[512,4096]{1,0:T(8,128)(2,1)} %param.5) | data formatting | bytes 8388608 | tf_op args[0]
  15.1 12.0 %all-to-all-start = ((bf16[128,32,512]{2,1,0:T(8,128)(2,1)}), bf16[128,32,512]{2,1,0:T(8,128)(2,1)}, u32[]{:S(2)}, u32[]{:S(2)}) async-start(bf16[128,32,512]{2,1,0:T(8,128)(2,1)} %bitcast.72), calls=%async_computation | async-start | bytes 8388608 | tf_op jit(solution)/shard_map/all_to_all | solution.py:27
  27.1 0.0 all-reduce.2.cloned.1.call-start
  27.2 0.1 broadcast_bitcast_fusion
  27.3 0.6 fusion.16
  29.8 1.8 broadcast_select_fusion
  31.5 0.9 bitcast_dynamic-update-slice_fusion.4
  32.5 1.0 bitcast_dynamic-update-slice_fusion.3
  33.4 0.9 bitcast_dynamic-update-slice_fusion.2
  34.3 0.9 bitcast_dynamic-update-slice_fusion.1
  35.3 0.9 bitcast_dynamic-update-slice_fusion
  36.2 0.9 fusion.7
  37.1 0.0 all-reduce.2.cloned.1.call-update
  37.1 0.0 all-gather.5.cloned.1.call-start
  44.7 46.7 %all-gather.3.cloned.1.call-done = bf16[2048,512]{1,0:T(8,128)(2,1)} async-done(((bf16[512,512]{1,0:T(8,128)(2,1)}), bf16[2048,512]{1,0:T(8,128)(2,1)}) %all-gather.3.cloned.1.call-update) | async-done | bytes 2097168 | tf_op jit(solution)/shard_map/all_gather | solution.py:37
  91.4 0.0 all-to-all-done
  91.4 1.3 convolution_convert_fusion.3
  92.7 133.6 %all-reduce.2.cloned.1.call-done = bf16[6,512,512]{2,1,0:T(8,128)(2,1)} async-done(((bf16[6,512,512]{2,1,0:T(8,128)(2,1)}), bf16[6,512,512]{2,1,0:T(8,128)(2,1)}) %all-reduce.2.cloned.1.call-update) | async-done | bytes 3145744 | tf_op jit(solution)/shard_map/psum | solution.py:36
  226.3 1.3 convolution_subtract_fusion.4
  227.6 1.6 convolution_convert_fusion.2
  229.3 1.3 convolution_subtract_fusion.2
  230.6 1.6 convolution_convert_fusion.1
  232.2 1.3 convolution_subtract_fusion.1
  233.6 1.6 convolution_convert_fusion
  235.2 0.7 pad_maximum_fusion
  235.9 0.0 all-gather.5.cloned.1.call-update
  235.9 79.1 %all-gather.5.cloned.1.call-done = bf16[4096,2048]{1,0:T(8,128)(2,1)} async-done(((bf16[32,2048]{1,0:T(8,128)(2,1)}), bf16[4096,2048]{1,0:T(8,128)(2,1)}) %all-gather.5.cloned.1.call-update) | async-done | bytes 16777232 | tf_op jit(solution)/shard_map/all_gather | solution.py:46
  315.1 1.1 dynamic-slice_bitcast_fusion
  316.2 0.8 copy.9
  317.0 14.4 %subtract_convert_fusion = bf16[512,4096]{1,0:T(8,128)(2,1)} fusion(bf16[512,4096]{1,0:T(8,128)(2,1)} %param.5, bf16[512,2048]{1,0:T(8,128)(2,1)S(1)} %broadcast_select_fusion, bf16[4096,2048]{1,0:T(8,128)(2,1)} %all-gather.5.cloned.1.call-done), kind=kOutput, calls=%fused_computation | convolution fusion | flops 8596226048 | bytes 27262976 | tf_op jit(solution)/shard_map/dot_general | solution.py:11
  (6 shorter events, 0.0 us)
Async XLA Ops:
  8.0 83.4 %all-gather.3.cloned.1.call-start = ((), (), s32[]{:S(2)}) async-start(), calls=%async_computation.1 | async-start | bytes 2621440 | tf_op jit(solution)/shard_map/all_gather | solution.py:37
  15.1 12.0 %copy-start.1 = (s32[1,4]{1,0:T(1,128)S(1)}, s32[1,4]{1,0:T(1,128)}, u32[]{:S(2)}) copy-start(s32[1,4]{1,0:T(1,128)} %param.8) | copy-start | bytes 52
  15.1 12.1 %copy-start = (s32[4]{0:T(128)S(1)}, s32[4]{0:T(128)}, u32[]{:S(2)}) copy-start(s32[4]{0:T(128)} %param.9) | copy-start | bytes 52
  15.1 76.2 %all-to-all-start = ((bf16[128,32,512]{2,1,0:T(8,128)(2,1)}), bf16[128,32,512]{2,1,0:T(8,128)(2,1)}, u32[]{:S(2)}, u32[]{:S(2)}) async-start(bf16[128,32,512]{2,1,0:T(8,128)(2,1)} %bitcast.72), calls=%async_computation | async-start | bytes 8388608 | tf_op jit(solution)/shard_map/all_to_all | solution.py:27
  27.1 199.2 %all-reduce.2.cloned.1.call-start = ((), (), s32[]{:S(2)}) async-start(), calls=%async_computation.2 | async-start | bytes 6291456 | tf_op jit(solution)/shard_map/psum | solution.py:36
  37.1 278.0 %all-gather.5.cloned.1.call-start = ((), (), s32[]{:S(2)}) async-start(), calls=%async_computation.3 | async-start | bytes 16908288 | tf_op jit(solution)/shard_map/all_gather | solution.py:46
Sparse Core Ops, SparseCore 0:
  10.6 80.7 all-gather.2
Sparse Core Ops, SparseCore 1:
  37.2 189.1 all-reduce.1
  236.0 79.0 all-gather.4
where the time goes:
time: 339 us
  waiting for transfers between devices  260 us (77%)
  between operations  25 us (7%)
  matrix products  24.5 us (7%)
  starting transfers between devices  12.1 us (4%)
  local copies, waits for them, and re-layouts  9 us (3%)
  other arithmetic  8.01 us (2%)
    psum x1, waiting for transfers between devices, body(): lower = lax.psum(jnp.stack(lower), AXES)  134 us
    all_gather x1, waiting for transfers between devices, body(): lax.all_gather(jnp.concatenate(solved, axis=1), AXES, axis=0, tiled=True)  79.1 us
    all_gather x1, waiting for transfers between devices, body(): lax.all_gather(diag_inverse, 'col', axis=0, tiled=True)  46.7 us
    dot_general x8, matrix products, dot_nt(): return lax.dot_general(a, b, NT, preferred_element_type=jnp.float32)  24.5 us
    all_to_all x1, starting transfers between devices, body(): lax.all_to_all(right_side.T.reshape(ndev, width, panel), AXES, split_axis...  12 us
    unnamed x8, local copies, waits for them, and re-layouts  7.29 us
  transfers between devices with their start and end apart: 4, of which 3 were waited for; matrix products, arithmetic and copies ran while one was open for 5% of the time, Pallas kernels for 0%

commit v1 on v0

--- a/solution.py
+++ b/solution.py
@@ -33,7 +33,7 @@
         for j in range(k):
             tile = masked[:, j * panel : (j + 1) * panel]
             lower.append(jnp.where(mine, tile, jnp.zeros_like(tile)))
-    lower = lax.psum(jnp.stack(lower), AXES)
+    lower = lax.psum(lax.psum(jnp.stack(lower), "col"), "row")
     inverses = lax.all_gather(diag_inverse, "col", axis=0, tiled=True).reshape(window, panel, panel)
     solved = []
     for k in range(window):

time: 339 us -> 402 us (1.19)
  waiting for transfers between devices: 260 us -> 323 us
    psum x1 -> x2, waiting for transfers between devices: 134 us -> 217 us  [body(): lower = lax.psum(lax.psum(jnp.stack(lower), 'col'), 'row')]
    all_gather x1, waiting for transfers between devices: 46.7 us -> 25 us  [body(): lax.all_gather(diag_inverse, 'col', axis=0, tiled=True)]
  transfers between devices with their start and end apart: 4 -> 5, of which waited for: 3 -> 4; matrix products, arithmetic and copies ran while one was open for 5% -> 2% of each run, Pallas kernels for 0% -> 0%
where the time goes in v1:
time: 402 us; the launch traced here: 401 us
  waiting for transfers between devices  323 us (80%)
  matrix products  24.5 us (6%)
  between operations  23.1 us (6%)
  starting transfers between devices  12.1 us (3%)
  local copies, waits for them, and re-layouts  9.79 us (2%)
  other arithmetic  8.63 us (2%)
    psum x2, waiting for transfers between devices, body(): lower = lax.psum(lax.psum(jnp.stack(lower), 'col'), 'row')  217 us
    all_gather x1, waiting for transfers between devices, body(): lax.all_gather(jnp.concatenate(solved, axis=1), AXES, axis=0, tiled=True)  80.7 us
    all_gather x1, waiting for transfers between devices, body(): lax.all_gather(diag_inverse, 'col', axis=0, tiled=True)  25 us
    dot_general x8, matrix products, dot_nt(): return lax.dot_general(a, b, NT, preferred_element_type=jnp.float32)  24.5 us
    all_to_all x1, starting transfers between devices, body(): lax.all_to_all(right_side.T.reshape(ndev, width, panel), AXES, split_axis...  12 us
  transfers between devices with their start and end apart: 5, of which 4 were waited for; matrix products, arithmetic and copies ran while one was open for 2% of the time, Pallas kernels for 0%

profile of v1, /device:TPU:1, one launch (start us, length us, event | category | flops | bytes accessed | tf_op | source)
XLA Modules:
  0.0 401.3 jit_solution(13019410600545195095)
XLA Ops:
  7.2 0.0 all-reduce.3.cloned.1.call-start
  7.2 1.4 fusion.16
  8.6 0.7 compare_bitcast_fusion
  9.3 0.1 broadcast_bitcast_fusion
  10.6 1.7 broadcast_select_fusion
  12.4 0.9 bitcast_dynamic-update-slice_fusion.4
  13.3 0.9 bitcast_dynamic-update-slice_fusion.3
  14.2 0.9 bitcast_dynamic-update-slice_fusion.2
  15.8 0.9 bitcast_dynamic-update-slice_fusion.1
  16.8 0.9 bitcast_dynamic-update-slice_fusion
  17.7 0.9 fusion.7
  18.6 0.0 all-gather.3.cloned.1.call-start
  18.6 0.7 all-gather.3.cloned.1.call-update
  19.3 6.4 %copy.8 = bf16[512,4096]{0,1:T(8,128)(2,1)} copy(bf16[512,4096]{1,0:T(8,128)(2,1)} %param.5) | data formatting | bytes 8388608 | tf_op args[0]
  25.7 12.0 %all-to-all-start = ((bf16[128,32,512]{2,1,0:T(8,128)(2,1)}), bf16[128,32,512]{2,1,0:T(8,128)(2,1)}, u32[]{:S(2)}, u32[]{:S(2)}) async-start(bf16[128,32,512]{2,1,0:T(8,128)(2,1)} %bitcast.72), calls=%async_computation | async-start | bytes 8388608 | tf_op jit(solution)/shard_map/all_to_all | solution.py:27
  37.7 0.0 all-reduce.5.cloned.1.call-start
  37.8 105.2 %all-reduce.3.cloned.1.call-done = bf16[6,512,512]{2,1,0:T(8,128)(2,1)} async-done(((bf16[6,512,512]{2,1,0:T(8,128)(2,1)}), bf16[6,512,512]{2,1,0:T(8,128)(2,1)}) %all-reduce.3.cloned.1.call-update) | async-done | bytes 3145744 | tf_op jit(solution)/shard_map/psum | solution.py:36
  143.0 0.0 all-gather.5.cloned.1.call-start
  150.4 25.0 %all-gather.3.cloned.1.call-done = bf16[2048,512]{1,0:T(8,128)(2,1)} async-done(((bf16[512,512]{1,0:T(8,128)(2,1)}), bf16[2048,512]{1,0:T(8,128)(2,1)}) %all-gather.3.cloned.1.call-update) | async-done | bytes 2097168 | tf_op jit(solution)/shard_map/all_gather | solution.py:37
  175.5 1.3 convolution_convert_fusion.3
  176.8 111.4 %all-reduce.5.cloned.1.call-done = bf16[6,512,512]{2,1,0:T(8,128)(2,1)} async-done(((bf16[6,512,512]{2,1,0:T(8,128)(2,1)}), bf16[6,512,512]{2,1,0:T(8,128)(2,1)}) %all-reduce.5.cloned.1.call-update) | async-done | bytes 3145744 | tf_op jit(solution)/shard_map/psum | solution.py:36
  288.1 1.3 convolution_subtract_fusion.4
  289.4 1.6 convolution_convert_fusion.2
  291.1 1.3 convolution_subtract_fusion.2
  292.4 1.6 convolution_convert_fusion.1
  294.0 1.3 convolution_subtract_fusion.1
  295.4 1.6 convolution_convert_fusion
  297.0 0.7 pad_maximum_fusion
  297.7 80.7 %all-gather.5.cloned.1.call-done = bf16[4096,2048]{1,0:T(8,128)(2,1)} async-done(((bf16[32,2048]{1,0:T(8,128)(2,1)}), bf16[4096,2048]{1,0:T(8,128)(2,1)}) %all-gather.5.cloned.1.call-update) | async-done | bytes 16777232 | tf_op jit(solution)/shard_map/all_gather | solution.py:46
  378.5 1.1 dynamic-slice_bitcast_fusion
  379.6 0.8 copy.9
  380.4 14.4 %subtract_convert_fusion = bf16[512,4096]{1,0:T(8,128)(2,1)} fusion(bf16[512,4096]{1,0:T(8,128)(2,1)} %param.5, bf16[512,2048]{1,0:T(8,128)(2,1)S(1)} %broadcast_select_fusion, bf16[4096,2048]{1,0:T(8,128)(2,1)} %all-gather.5.cloned.1.call-done), kind=kOutput, calls=%fused_computation | convolution fusion | flops 8596226048 | bytes 27262976 | tf_op jit(solution)/shard_map/dot_general | solution.py:11
  (5 shorter events, 0.1 us)
Async XLA Ops:
  7.2 135.8 %all-reduce.3.cloned.1.call-start = ((), (), s32[]{:S(2)}) async-start(), calls=%async_computation.2 | async-start | bytes 6291456 | tf_op jit(solution)/shard_map/psum | solution.py:36
  18.6 156.9 %all-gather.3.cloned.1.call-start = ((), (), s32[]{:S(2)}) async-start(), calls=%async_computation.1 | async-start | bytes 2621440 | tf_op jit(solution)/shard_map/all_gather | solution.py:37
  25.7 149.7 %all-to-all-start = ((bf16[128,32,512]{2,1,0:T(8,128)(2,1)}), bf16[128,32,512]{2,1,0:T(8,128)(2,1)}, u32[]{:S(2)}, u32[]{:S(2)}) async-start(bf16[128,32,512]{2,1,0:T(8,128)(2,1)} %bitcast.72), calls=%async_computation | async-start | bytes 8388608 | tf_op jit(solution)/shard_map/all_to_all | solution.py:27
  37.7 250.4 %all-reduce.5.cloned.1.call-start = ((), (), s32[]{:S(2)}) async-start(), calls=%async_computation.3 | async-start | bytes 6291456 | tf_op jit(solution)/shard_map/psum | solution.py:36
  143.0 235.5 %all-gather.5.cloned.1.call-start = ((), (), s32[]{:S(2)}) async-start(), calls=%async_computation.4 | async-start | bytes 16908288 | tf_op jit(solution)/shard_map/all_gather | solution.py:46
Sparse Core Ops, SparseCore 0:
  18.7 124.2 all-reduce.2
  144.7 30.7 all-gather.2
  178.8 109.2 all-reduce.4
  297.9 80.5 all-gather.4

commit v2 on v0

--- a/solution.py
+++ b/solution.py
@@ -34,7 +34,9 @@
             tile = masked[:, j * panel : (j + 1) * panel]
             lower.append(jnp.where(mine, tile, jnp.zeros_like(tile)))
     lower = lax.psum(jnp.stack(lower), AXES)
-    inverses = lax.all_gather(diag_inverse, "col", axis=0, tiled=True).reshape(window, panel, panel)
+    inverses = jnp.concatenate(
+        lax.all_to_all(jnp.stack([diag_inverse] * lax.axis_size("col")), "col", 0, 0), axis=0
+    ).reshape(window, panel, panel)
     solved = []
     for k in range(window):
         residual = lax.dynamic_index_in_dim(pieces, window_rows[k], 0, keepdims=False).astype(

time: 339 us -> 351 us (1.035)
  waiting for transfers between devices: 260 us -> 266 us
  local copies, waits for them, and re-layouts: 9 us -> 12.8 us
    all_gather x1 -> x0, waiting for transfers between devices: 46.7 us -> none  [body(): lax.all_gather(diag_inverse, 'col', axis=0, tiled=True)]
    all_to_all x1, waiting for transfers between devices: 0.01 us -> 37.3 us  [body(): lax.all_to_all(right_side.T.reshape(ndev, width, panel), AXES, split_axis...]
    all_to_all x0 -> x1, waiting for transfers between devices: none -> 19 us  [body(): lax.all_to_all(jnp.stack([diag_inverse] * lax.axis_size('col')), 'col', 0...]
    all_to_all x0 -> x1, starting transfers between devices: none -> 5.86 us  [body(): lax.all_to_all(jnp.stack([diag_inverse] * lax.axis_size('col')), 'col', 0...]
    unnamed x8 -> x10, local copies, waits for them, and re-layouts: 7.29 us -> 8.6 us
  transfers between devices with their start and end apart: 4 -> 4, of which waited for: 3 -> 4; matrix products, arithmetic and copies ran while one was open for 5% -> 4% of each run, Pallas kernels for 0% -> 0%
where the time goes in v2:
time: 351 us; the launch traced here: 350 us
  waiting for transfers between devices  266 us (76%)
  matrix products  24.5 us (7%)
  between operations  23.6 us (7%)
  starting transfers between devices  15.4 us (4%)
  local copies, waits for them, and re-layouts  12.8 us (4%)
  other arithmetic  7.98 us (2%)
    psum x1, waiting for transfers between devices, body(): lower = lax.psum(jnp.stack(lower), AXES)  130 us
    all_gather x1, waiting for transfers between devices, body(): lax.all_gather(jnp.concatenate(solved, axis=1), AXES, axis=0, tiled=True)  79.3 us
    all_to_all x1, waiting for transfers between devices, body(): lax.all_to_all(right_side.T.reshape(ndev, width, panel), AXES, split_axis...  37.3 us
    dot_general x8, matrix products, dot_nt(): return lax.dot_general(a, b, NT, preferred_element_type=jnp.float32)  24.5 us
    all_to_all x1, waiting for transfers between devices, body(): lax.all_to_all(jnp.stack([diag_inverse] * lax.axis_size('col')), 'col', 0...  19 us
    all_to_all x1, starting transfers between devices, body(): lax.all_to_all(right_side.T.reshape(ndev, width, panel), AXES, split_axis...  9.45 us
    unnamed x10, local copies, waits for them, and re-layouts  8.6 us
  transfers between devices with their start and end apart: 4, of which 4 were waited for; matrix products, arithmetic and copies ran while one was open for 4% of the time, Pallas kernels for 0%

profile of v2, /device:TPU:1, one launch (start us, length us, event | category | flops | bytes accessed | tf_op | source)
XLA Modules:
  0.0 350.4 jit_solution(7928867839564084833)
XLA Ops:
  7.2 2.5 stack.28
  9.7 5.9 %all-to-all-start.1 = ((bf16[4,512,512]{2,1,0:T(8,128)(2,1)}), bf16[4,512,512]{2,1,0:T(8,128)(2,1)S(1)}, u32[]{:S(2)}, u32[]{:S(2)}) async-start(bf16[4,512,512]{2,1,0:T(8,128)(2,1)} %stack.28), calls=%async_computation.1 | async-start | bytes 4194304 | tf_op jit(solution)/shard_map/all_to_all | solution.py:38
  15.6 6.4 %copy.8 = bf16[512,4096]{0,1:T(8,128)(2,1)} copy(bf16[512,4096]{1,0:T(8,128)(2,1)} %param.5) | data formatting | bytes 8388608 | tf_op args[0]
  22.0 19.0 %all-to-all-done.1 = bf16[4,512,512]{2,1,0:T(8,128)(2,1)S(1)} async-done(((bf16[4,512,512]{2,1,0:T(8,128)(2,1)}), bf16[4,512,512]{2,1,0:T(8,128)(2,1)S(1)}, u32[]{:S(2)}, u32[]{:S(2)}) %all-to-all-start.1) | async-done | bytes 2097184 | tf_op jit(solution)/shard_map/all_to_all | solution.py:38
  41.0 1.3 copy-done
  42.3 9.4 %all-to-all-start = ((bf16[128,32,512]{2,1,0:T(8,128)(2,1)}), bf16[128,32,512]{2,1,0:T(8,128)(2,1)}, u32[]{:S(2)}, u32[]{:S(2)}) async-start(bf16[128,32,512]{2,1,0:T(8,128)(2,1)} %bitcast.84), calls=%async_computation | async-start | bytes 8388608 | tf_op jit(solution)/shard_map/all_to_all | solution.py:27
  51.8 0.0 all-reduce.2.cloned.1.call-start
  51.8 0.1 broadcast_bitcast_fusion
  51.9 0.6 fusion.12
  54.4 1.7 broadcast_select_fusion
  56.2 0.9 bitcast_dynamic-update-slice_fusion.4
  57.1 1.0 bitcast_dynamic-update-slice_fusion.3
  58.0 0.9 bitcast_dynamic-update-slice_fusion.2
  59.0 0.9 bitcast_dynamic-update-slice_fusion.1
  59.9 0.9 bitcast_dynamic-update-slice_fusion
  60.8 0.9 fusion.4
  61.7 0.0 all-reduce.2.cloned.1.call-update
  61.7 0.0 all-gather.2.cloned.1.call-start
  69.3 37.3 %all-to-all-done = bf16[128,32,512]{2,1,0:T(8,128)(2,1)} async-done(((bf16[128,32,512]{2,1,0:T(8,128)(2,1)}), bf16[128,32,512]{2,1,0:T(8,128)(2,1)}, u32[]{:S(2)}, u32[]{:S(2)}) %all-to-all-start) | async-done | bytes 4194336 | tf_op jit(solution)/shard_map/all_to_all | solution.py:27
  106.6 1.3 convolution_convert_fusion.3
  107.9 130.5 %all-reduce.2.cloned.1.call-done = bf16[6,512,512]{2,1,0:T(8,128)(2,1)} async-done(((bf16[6,512,512]{2,1,0:T(8,128)(2,1)}), bf16[6,512,512]{2,1,0:T(8,128)(2,1)}) %all-reduce.2.cloned.1.call-update) | async-done | bytes 3145744 | tf_op jit(solution)/shard_map/psum | solution.py:36
  238.4 1.3 convolution_subtract_fusion.4
  239.7 1.6 convolution_convert_fusion.2
  241.4 1.3 convolution_subtract_fusion.2
  242.7 1.6 convolution_convert_fusion.1
  244.3 1.3 convolution_subtract_fusion.1
  245.7 1.6 convolution_convert_fusion
  247.3 0.7 pad_maximum_fusion
  248.0 79.3 %all-gather.2.cloned.1.call-done = bf16[4096,2048]{1,0:T(8,128)(2,1)} async-done(((bf16[32,2048]{1,0:T(8,128)(2,1)}), bf16[4096,2048]{1,0:T(8,128)(2,1)}) %all-gather.2.cloned.1.call-update) | async-done | bytes 16777232 | tf_op jit(solution)/shard_map/all_gather | solution.py:48
  327.3 1.1 dynamic-slice_bitcast_fusion
  328.4 0.8 copy.9
  329.2 14.4 %subtract_convert_fusion = bf16[512,4096]{1,0:T(8,128)(2,1)} fusion(bf16[512,4096]{1,0:T(8,128)(2,1)} %param.5, bf16[512,2048]{1,0:T(8,128)(2,1)S(1)} %broadcast_select_fusion, bf16[4096,2048]{1,0:T(8,128)(2,1)} %all-gather.2.cloned.1.call-done), kind=kOutput, calls=%fused_computation | convolution fusion | flops 8596226048 | bytes 27262976 | tf_op jit(solution)/shard_map/dot_general | solution.py:11
  (8 shorter events, 0.0 us)
Async XLA Ops:
  9.7 31.3 %all-to-all-start.1 = ((bf16[4,512,512]{2,1,0:T(8,128)(2,1)}), bf16[4,512,512]{2,1,0:T(8,128)(2,1)S(1)}, u32[]{:S(2)}, u32[]{:S(2)}) async-start(bf16[4,512,512]{2,1,0:T(8,128)(2,1)} %stack.28), calls=%async_computation.1 | async-start | bytes 4194304 | tf_op jit(solution)/shard_map/all_to_all | solution.py:38
  41.0 1.3 copy-start
  41.0 10.8 %copy-start.2 = (s32[1,4]{1,0:T(1,128)S(1)}, s32[1,4]{1,0:T(1,128)}, u32[]{:S(2)}) copy-start(s32[1,4]{1,0:T(1,128)} %param.8) | copy-start | bytes 52
  41.0 10.9 %copy-start.1 = (s32[4]{0:T(128)S(1)}, s32[4]{0:T(128)}, u32[]{:S(2)}) copy-start(s32[4]{0:T(128)} %param.9) | copy-start | bytes 52
  42.3 64.3 %all-to-all-start = ((bf16[128,32,512]{2,1,0:T(8,128)(2,1)}), bf16[128,32,512]{2,1,0:T(8,128)(2,1)}, u32[]{:S(2)}, u32[]{:S(2)}) async-start(bf16[128,32,512]{2,1,0:T(8,128)(2,1)} %bitcast.84), calls=%async_computation | async-start | bytes 8388608 | tf_op jit(solution)/shard_map/all_to_all | solution.py:27
  51.8 186.7 %all-reduce.2.cloned.1.call-start = ((), (), s32[]{:S(2)}) async-start(), calls=%async_computation.2 | async-start | bytes 6291456 | tf_op jit(solution)/shard_map/psum | solution.py:36
  61.7 265.6 %all-gather.2.cloned.1.call-start = ((), (), s32[]{:S(2)}) async-start(), calls=%async_computation.3 | async-start | bytes 16908288 | tf_op jit(solution)/shard_map/all_gather | solution.py:48
Sparse Core Ops, SparseCore 0:
  61.9 176.5 all-reduce.1
  248.1 79.0 all-gather.1
